TPU v7x, 32 devices: a whole 2x2x4 slice. The times are simulated.
32 devices in a mesh: seq: 16 (over z, y, x), tensor: 2 (over core).
Axes of the slice: x: 2, y: 2, z: 4, core: 2. Of those that a mesh axis runs over, the one named last changes fastest.
Arguments:
- tokens: bfloat16 [1024, 4096], P('seq', 'tensor'), may hold values from -6 to 6
- w_gate: bfloat16 [16, 4096, 4096], P('seq', None, 'tensor'), may hold values from -0.09375 to 0.09375
- w_up: bfloat16 [16, 4096, 4096], P('seq', None, 'tensor'), may hold values from -0.09375 to 0.09375
- w_down: bfloat16 [16, 4096, 4096], P('seq', None, 'tensor'), may hold values from -0.0625 to 0.0625
- routes: int32 [8, 2], replicated, may hold values from 0 to 7, all different within a row; in each aligned block of 8 rows (0 to 7, 8 to 15, ...) at most 3 rows name the same one
- gate_values: float32 [8, 2], replicated, may hold values from 0.1 to 0.9
Outputs:
- moe_out: bfloat16 [1024, 4096], P('seq', 'tensor')
Inputs may be any that keep to these rules, and one draw needn't show every extreme that they name: `routes`: the two experts of a block differ; every expert is named by some block and by at most 3 blocks, and one by exactly 3.
All inputs are finite; a program needn't handle non-finite values.
Results may differ from a plain program's by a relative error of at most 0.005.
Values may be sent and summed in bfloat16 or wider, within the bound.
No kernel may reach another device: no remote copies, remote signals or barrier semaphores. Data moves between devices by JAX's collectives and lax.ppermute only.
A program may use at most 128 MiB of HBM per device.

v0:
```python
import jax
import jax.numpy as jnp
from jax import lax
from jax.sharding import PartitionSpec as P

E = 8


def route_slots(routes, gate_values, expert, capacity):
    block_count = routes.shape[0]
    matches = routes == expert
    member = jnp.any(matches, axis=1).astype(jnp.int32)
    weight = jnp.sum(jnp.where(matches, gate_values, 0.0), axis=1)
    position = jnp.cumsum(member) - 1
    slot_ids = jnp.arange(capacity, dtype=jnp.int32)
    picked = (member[None, :] == 1) & (position[None, :] == slot_ids[:, None])
    block_ids = jnp.arange(block_count, dtype=jnp.int32)
    block_index = jnp.sum(jnp.where(picked, block_ids[None, :], 0), axis=1)
    slot_gate = jnp.sum(jnp.where(picked, weight[None, :], 0.0), axis=1)
    return (picked, block_index, slot_gate)


def per_device(tokens, w_gate, w_up, w_down, routes, gate_values):
    seq_count = lax.axis_size("seq")
    part_count = seq_count // E
    expert = lax.axis_index("seq") // part_count
    block_count = routes.shape[0]
    capacity = 3 * block_count // 8
    columns = lax.all_gather(tokens, "seq", axis=0, tiled=True)
    block_rows = columns.shape[0] // block_count
    feature_width = columns.shape[1]
    picked, block_index, slot_gate = route_slots(routes, gate_values, expert, capacity)
    chosen = columns.reshape(block_count, block_rows, feature_width)[block_index]
    chosen = chosen.reshape(capacity * block_rows, feature_width)
    gate_cols = w_gate[0]
    up_cols = w_up[0]
    full_rows = lax.all_gather(chosen, "tensor", axis=1, tiled=True)
    gate_sum = jnp.dot(full_rows, gate_cols, preferred_element_type=jnp.float32)
    up_sum = jnp.dot(full_rows, up_cols, preferred_element_type=jnp.float32)
    hidden = (jax.nn.silu(gate_sum) * up_sum).astype(jnp.bfloat16)
    quarter = lax.all_gather(hidden, "tensor", axis=1, tiled=True)
    partial_value = jnp.dot(quarter, w_down[0], preferred_element_type=jnp.float32)
    weighted = partial_value.reshape(capacity, block_rows, feature_width) * slot_gate[:, None, None]
    scattered = jnp.einsum(
        "lb,lrd->brd", picked.astype(jnp.float32), weighted, precision=lax.Precision.HIGHEST
    )
    scattered = scattered.reshape(block_count * block_rows, feature_width)
    summed = lax.psum_scatter(scattered, "seq", scatter_dimension=0, tiled=True)
    return summed.astype(jnp.bfloat16)


def solution(mesh):
    placed = (
        P("seq", "tensor"),
        P("seq", None, "tensor"),
        P("seq", None, "tensor"),
        P("seq", None, "tensor"),
        P(),
        P(),
    )
    return jax.shard_map(
        per_device, mesh=mesh, in_specs=placed, out_specs=P("seq", "tensor"), check_vma=False
    )
```

profile of v0, /device:TPU:10, one launch (start us, length us, event | category | flops | bytes accessed | tf_op | source)
XLA Modules:
  0.0 356.7 jit_solution(6207690128557403853)
XLA Ops:
  6.5 0.0 all-gather.4.cloned.1.call-start
  6.5 0.7 all-gather.4.cloned.1.call-update
  7.3 0.0 all-gather.6.cloned.1.call-start
  7.3 0.7 fusion.13
  8.0 0.2 reduce-window.8
  8.2 0.1 select_reduce_fusion.1
  8.4 78.5 %all-gather.4.cloned.1.call-done = bf16[1024,2048]{1,0:T(8,128)(2,1)} async-done(((bf16[64,2048]{1,0:T(8,128)(2,1)}), bf16[1024,2048]{1,0:T(8,128)(2,1)}) %all-gather.4.cloned.1.call-update) | async-done | bytes 4194320 | tf_op jit(solution)/shard_map/all_gather | solution.py:29
  86.8 4.1 %gather_fusion = bf16[3,128,2048]{2,1,0:T(8,128)(2,1)} fusion(bf16[8,128,2048]{2,1,0:T(8,128)(2,1)} %bitcast.32, s32[1024]{0:T(1024)S(1)} %pad_clamp_fusion), kind=kCustom, calls=%fused_computation | custom fusion | bytes 3145740 | tf_op jit(solution)/shard_map/gather | solution.py:33
  90.9 0.0 all-gather.6.cloned.1.call-update
  90.9 0.0 all-gather.8.cloned.1.call-start
  91.0 11.1 %all-gather.6.cloned.1.call-done = bf16[384,4096]{1,0:T(8,128)(2,1)} async-done(((bf16[384,2048]{1,0:T(8,128)(2,1)}), bf16[384,4096]{1,0:T(8,128)(2,1)}) %all-gather.6.cloned.1.call-update) | async-done | bytes 3145744 | tf_op jit(solution)/shard_map/all_gather | solution.py:37
  102.1 0.0 copy-start.2
  102.1 13.2 %fusion.4 = f32[384,2048]{1,0:T(8,128)S(1)} fusion(bf16[384,4096]{1,0:T(8,128)(2,1)} %all-gather.6.cloned.1.call-done, bf16[1,4096,2048]{2,1,0:T(8,128)(2,1)} %param.7), kind=kOutput, calls=%fused_computation.5 | convolution fusion | flops 6442450944 | bytes 23068672 | tf_op jit(solution)/shard_map/dot_general | solution.py:38
  115.3 0.0 copy-done.2
  115.3 0.0 copy-start
  115.3 0.0 copy-start.1
  115.3 11.3 %multiply_convert_fusion = bf16[384,2048]{1,0:T(8,128)(2,1)} fusion(f32[384,2048]{1,0:T(8,128)S(1)} %fusion.4, bf16[384,4096]{1,0:T(8,128)(2,1)S(1)} %copy-done.2, bf16[1,4096,2048]{2,1,0:T(8,128)(2,1)} %param.8), kind=kOutput, calls=%fused_computation.9 | convolution fusion | flops 6447169536 | bytes 24641536 | tf_op jit(solution)/shard_map/dot_general | solution.py:39
  126.7 0.0 all-gather.8.cloned.1.call-update
  126.7 0.0 reduce-scatter.2.cloned.1.call-start
  126.8 0.0 copy-done
  126.8 0.0 copy-done.1
  126.8 0.1 select_reduce_fusion
  126.9 13.2 %all-gather.8.cloned.1.call-done = bf16[384,4096]{1,0:T(8,128)(2,1)} async-done(((bf16[384,2048]{1,0:T(8,128)(2,1)}), bf16[384,4096]{1,0:T(8,128)(2,1)}) %all-gather.8.cloned.1.call-update) | async-done | bytes 3145744 | tf_op jit(solution)/shard_map/all_gather | solution.py:41
  140.2 11.3 %fusion = f32[3,128,2048]{2,1,0:T(8,128)S(1)} fusion(bf16[3,128,4096]{2,1,0:T(8,128)(2,1)} %bitcast.33, bf16[1,4096,2048]{2,1,0:T(8,128)(2,1)} %param.9), kind=kOutput, calls=%fused_computation.1 | convolution fusion | flops 6442450944 | bytes 23068672 | tf_op jit(solution)/shard_map/dot_general | solution.py:42
  151.5 6.7 %fusion.6 = f32[8,128,2048]{2,0,1:T(8,128)S(1)} fusion(f32[3,128,2048]{2,1,0:T(8,128)S(1)} %fusion, f32[3]{0:T(128)S(1)} %select_reduce_fusion, s32[8]{0:T(128)S(1)} %add_bitcast_fusion, pred[8]{0:T(512)(128)(4,1)S(1)} %get-tuple-element.5), kind=kOutput, calls=%fused_computation.8 | convolution fusion | flops 76283952 | bytes 11534388 | tf_op jit(solution)/shard_map/lb,lrd->brd/dot_general | solution.py:44
  158.2 8.1 %copy.7 = f32[8,128,2048]{2,1,0:T(8,128)} copy(f32[8,128,2048]{2,0,1:T(8,128)S(1)} %fusion.6) | data formatting | bytes 16777216 | tf_op jit(solution)/shard_map/lb,lrd->brd/dot_general | solution.py:44
  166.3 0.0 reduce-scatter.2.cloned.1.call-update
  166.3 182.1 %reduce-scatter.2.cloned.1.call-done = f32[64,2048]{1,0:T(8,128)} async-done(((f32[1024,2048]{1,0:T(8,128)}), f32[64,2048]{1,0:T(8,128)}) %reduce-scatter.2.cloned.1.call-update) | async-done | bytes 524304 | tf_op jit(solution)/shard_map/reduce_scatter | solution.py:48
  348.4 1.8 convert_element_type.32
  (5 shorter events, 0.1 us)
Async XLA Ops:
  6.5 80.3 %all-gather.4.cloned.1.call-start = ((), (), s32[]{:S(2)}) async-start(), calls=%async_computation.1 | async-start | bytes 4456448 | tf_op jit(solution)/shard_map/all_gather | solution.py:29
  7.3 94.8 %all-gather.6.cloned.1.call-start = ((), (), s32[]{:S(2)}) async-start(), calls=%async_computation.2 | async-start | bytes 4718592 | tf_op jit(solution)/shard_map/all_gather | solution.py:37
  90.9 49.2 %all-gather.8.cloned.1.call-start = ((), (), s32[]{:S(2)}) async-start(), calls=%async_computation.3 | async-start | bytes 4718592 | tf_op jit(solution)/shard_map/all_gather | solution.py:41
  102.1 13.2 %copy-start.2 = (bf16[384,4096]{1,0:T(8,128)(2,1)S(1)}, bf16[384,4096]{1,0:T(8,128)(2,1)}, u32[]{:S(2)}) copy-start(bf16[384,4096]{1,0:T(8,128)(2,1)} %all-gather.6.cloned.1.call-done) | copy-start | bytes 9437188
  115.3 11.5 %copy-start = (s32[8,2]{0,1:T(2,128)S(1)}, s32[8,2]{0,1:T(2,128)}, u32[]{:S(2)}) copy-start(s32[8,2]{0,1:T(2,128)} %param.10) | copy-start | bytes 196
  115.3 11.4 %copy-start.1 = (f32[8,2]{0,1:T(2,128)S(1)}, f32[8,2]{0,1:T(2,128)}, u32[]{:S(2)}) copy-start(f32[8,2]{0,1:T(2,128)} %param.11) | copy-start | bytes 196
  126.7 221.7 %reduce-scatter.2.cloned.1.call-start = ((), (), s32[]{:S(2)}) async-start(), calls=%async_computation.4 | async-start | bytes 8912896 | tf_op jit(solution)/shard_map/reduce_scatter | solution.py:48
Sparse Core Ops, SparseCore 0:
  10.1 76.6 all-gather.3
  91.0 10.9 all-gather.5
  126.8 13.2 all-gather.7
  166.4 181.9 reduce-scatter.1
where the time goes:
time: 357 us
  waiting for transfers between devices  286 us (80%)
  matrix products  42.6 us (12%)
  between operations  13.2 us (4%)
  local copies, waits for them, and re-layouts  12.2 us (3%)
    reduce_scatter x1, waiting for transfers between devices, per_device(): summed = lax.psum_scatter(scattered, 'seq', scatter_dimension=0, tiled=True)  182 us
    all_gather x1, waiting for transfers between devices, per_device(): columns = lax.all_gather(tokens, 'seq', axis=0, tiled=True)  78.5 us
    all_gather x1, waiting for transfers between devices, per_device(): quarter = lax.all_gather(hidden, 'tensor', axis=1, tiled=True)  13.2 us
    dot_general x1, matrix products, per_device(): gate_sum = jnp.dot(full_rows, gate_cols, preferred_element_type=jnp.float32)  13.2 us
    dot_general x1, matrix products, per_device(): up_sum = jnp.dot(full_rows, up_cols, preferred_element_type=jnp.float32)  11.3 us
    dot_general x1, matrix products, per_device(): jnp.dot(quarter, w_down[0], preferred_element_type=jnp.float32)  11.3 us
    all_gather x1, waiting for transfers between devices, per_device(): full_rows = lax.all_gather(chosen, 'tensor', axis=1, tiled=True)  11.1 us
    dot_general x1, local copies, waits for them, and re-layouts, per_device(): jnp.einsum('lb,lrd->brd', picked.astype(jnp.float32), weighted, precision...  8.08 us
  transfers between devices with their start and end apart: 4, of which 4 were waited for; matrix products, arithmetic and copies ran while one was open for 0% of the time, Pallas kernels for 0%

commit v1 on v0

v1 whole, which is shorter than its diff:
```python
import jax
import jax.numpy as jnp
from jax import lax
from jax.experimental import pallas as pl
from jax.experimental.pallas import tpu as pltpu
from jax.sharding import PartitionSpec as P


E = 8
BF16 = jnp.bfloat16
F32 = jnp.float32
D_CHUNKS = 2
C_CHUNKS = 2


def route_slots(routes, gate_values, expert, capacity):
    block_count = routes.shape[0]
    matches = routes == expert
    member = jnp.any(matches, axis=1).astype(jnp.int32)
    weight = jnp.sum(jnp.where(matches, gate_values, 0.0), axis=1)
    position = jnp.cumsum(member) - 1
    slot_ids = jnp.arange(capacity, dtype=jnp.int32)
    picked = (member[None, :] == 1) & (position[None, :] == slot_ids[:, None])
    block_ids = jnp.arange(block_count, dtype=jnp.int32)
    block_index = jnp.sum(jnp.where(picked, block_ids[None, :], 0), axis=1)
    slot_gate = jnp.sum(jnp.where(picked, weight[None, :], 0.0), axis=1)
    return (picked, block_index, slot_gate)


def gathered(tokens, w_gate, w_up, w_down, routes, gate_values):
    seq_count = lax.axis_size("seq")
    part_count = seq_count // E
    expert = lax.axis_index("seq") // part_count
    block_count = routes.shape[0]
    capacity = 3 * block_count // 8
    columns = lax.all_gather(tokens, "seq", axis=0, tiled=True)
    block_rows = columns.shape[0] // block_count
    feature_width = columns.shape[1]
    picked, block_index, slot_gate = route_slots(routes, gate_values, expert, capacity)
    chosen = columns.reshape(block_count, block_rows, feature_width)[block_index]
    chosen = chosen.reshape(capacity * block_rows, feature_width)
    full_rows = lax.all_gather(chosen, "tensor", axis=1, tiled=True)
    gate_sum = jnp.dot(full_rows, w_gate[0], preferred_element_type=F32)
    up_sum = jnp.dot(full_rows, w_up[0], preferred_element_type=F32)
    hidden = (jax.nn.silu(gate_sum) * up_sum).astype(BF16)
    quarter = lax.all_gather(hidden, "tensor", axis=1, tiled=True)
    partial_value = jnp.dot(quarter, w_down[0], preferred_element_type=F32)
    weighted = partial_value.reshape(capacity, block_rows, feature_width) * slot_gate[:, None, None]
    scattered = jnp.einsum(
        "lb,lrd->brd", picked.astype(F32), weighted, precision=lax.Precision.HIGHEST
    )
    scattered = scattered.reshape(block_count * block_rows, feature_width)
    summed = lax.psum_scatter(scattered, "seq", scatter_dimension=0, tiled=True)
    return summed.astype(BF16)


def params(mebibytes=4):
    return pltpu.CompilerParams(vmem_limit_bytes=mebibytes << 20)


def tables(routes, gate_values, lines, pairs, halves, capacity):
    block_count = routes.shape[0]
    size = 2 * capacity + 2 * lines + 1

    def kernel(routes_ref, values_ref, place_ref, gate_ref):
        me = lax.axis_index("seq")
        expert = me // halves
        z, y = expert // pairs, expert % pairs
        for l in range(capacity):
            place_ref[l] = 0
            place_ref[capacity + l] = 0
            gate_ref[l] = 0.0
        for k in range(2 * lines):
            place_ref[2 * capacity + k] = capacity
        place_ref[size - 1] = lax.axis_index("tensor")
        for side in range(2):
            wanted = expert if side == 0 else expert ^ 1
            count = jnp.int32(0)
            for b in range(block_count):
                first, second = routes_ref[b, 0] == wanted, routes_ref[b, 1] == wanted
                named = jnp.logical_or(first, second)
                here = y == b % pairs
                place = (z - b // pairs + lines) % lines
                slot = jnp.minimum(count, capacity - 1)

                @pl.when(named)
                def _():
                    if side == 0:
                        place_ref[slot] = jnp.where(here, place, lines)
                        gate_ref[slot] = jnp.where(first, values_ref[b, 0], values_ref[b, 1])
                    else:
                        place_ref[capacity + slot] = place

                    @pl.when(here)
                    def _():
                        place_ref[2 * capacity + 2 * ((lines - place) % lines) + side] = slot

                count = count + named.astype(jnp.int32)

    scalar = pl.BlockSpec(memory_space=pltpu.SMEM)
    return pl.pallas_call(
        kernel,
        out_shape=[
            jax.ShapeDtypeStruct((size,), jnp.int32),
            jax.ShapeDtypeStruct((capacity,), F32),
        ],
        in_specs=[scalar, scalar],
        out_specs=[scalar, scalar],
        compiler_params=params(),
    )(routes, gate_values)


INSIDE = pl.BlockSpec(memory_space=pltpu.VMEM)
SCALAR = pl.BlockSpec(memory_space=pltpu.SMEM)


def pick(sources, places, first, capacity, rows, came=None):
    width = sources[0].shape[1]
    extra = [] if came is None else [came]

    def kernel(place_ref, *refs):
        out_ref = refs[-1]
        for l in range(capacity):
            here = pl.ds(l * rows, rows)
            for s, ref in enumerate(refs[: len(sources)]):

                @pl.when(place_ref[first + l] == s)
                def _():
                    out_ref[here, :] = ref[...]

            if came is not None:

                @pl.when(place_ref[first + l] == len(sources))
                def _():
                    out_ref[here, :] = refs[len(sources)][here, :]

    size = capacity * rows * width
    return pl.pallas_call(
        kernel,
        out_shape=jax.ShapeDtypeStruct((capacity * rows, width), BF16),
        in_specs=[SCALAR] + [INSIDE] * (len(sources) + len(extra)),
        out_specs=INSIDE,
        cost_estimate=pl.CostEstimate(flops=size, bytes_accessed=6 * size, transcendentals=0),
        compiler_params=params(),
    )(places, *sources, *extra)


def gate_up(pieces, w_gate, w_up, places, chunk, tile, sums=()):
    half, step = pieces[0].shape
    rows = 2 * half
    depth, width = w_gate.shape
    per_side = depth // 2 // step
    final = chunk == per_side - 1
    last = places.shape[0] - 1
    count = len(sums)

    def kernel(place_ref, own_ref, far_ref, mate_ref, mate_far_ref, g0, g1, u0, u1, *refs):
        sum_refs, out_refs, x_ref = refs[:count], refs[count:-1], refs[-1]

        @pl.when(pl.program_id(0) == 0)
        def _():
            x_ref[:half, :step] = own_ref[...]
            x_ref[:half, step:] = far_ref[...]
            x_ref[half:, :step] = mate_ref[...]
            x_ref[half:, step:] = mate_far_ref[...]

        def dot(ref0, ref1):
            return jnp.dot(
                x_ref[:, :step], ref0[...], preferred_element_type=F32
            ) + jnp.dot(x_ref[:, step:], ref1[...], preferred_element_type=F32)

        gate, up = dot(g0, g1), dot(u0, u1)
        if sum_refs:
            gate, up = gate + sum_refs[0][...], up + sum_refs[1][...]
        if final:
            out_refs[0][...] = (gate / (1.0 + jnp.exp(-gate)) * up).astype(BF16)
        else:
            out_refs[0][...], out_refs[1][...] = gate, up

    near_rows = pl.BlockSpec((step, tile), lambda i, p: (p[last] * per_side + chunk, i))
    far_rows = pl.BlockSpec((step, tile), lambda i, p: ((1 - p[last]) * per_side + chunk, i))
    column = pl.BlockSpec((rows, tile), lambda i, p: (0, i))
    wide = jax.ShapeDtypeStruct((rows, width), F32)
    return pl.pallas_call(
        kernel,
        out_shape=jax.ShapeDtypeStruct((rows, width), BF16) if final else [wide, wide],
        grid_spec=pltpu.PrefetchScalarGridSpec(
            num_scalar_prefetch=1,
            grid=(width // tile,),
            in_specs=[pl.BlockSpec(a.shape, lambda i, p: (0, 0)) for a in pieces]
            + [near_rows, far_rows, near_rows, far_rows]
            + [column] * count,
            out_specs=column if final else [column, column],
            scratch_shapes=[pltpu.VMEM((rows, 2 * step), BF16)],
        ),
        cost_estimate=pl.CostEstimate(
            flops=8 * rows * step * width,
            bytes_accessed=8 * step * width + 4 * rows * step + 8 * rows * width,
            transcendentals=rows * width if final else 0,
        ),
        compiler_params=params(44),
    )(places, *pieces, w_gate, w_gate, w_up, w_up, *sums)


def down(hidden, far, w_down, places, gates, tile, first, width):
    streamed = w_down.shape[1] > width
    rows, half = hidden.shape
    capacity = gates.shape[0]
    part = rows // 2 // capacity

    def kernel(place_ref, gate_ref, own_ref, far_ref, w_ref, keep_ref, send_ref):
        core = place_ref[places.shape[0] - 1]
        here = pl.multiple_of(core * half, half)
        there = pl.multiple_of((1 - core) * half, half)
        for i in range(1 if streamed else width // tile):
            columns = slice(i * tile, (i + 1) * tile)
            total = jnp.dot(
                own_ref[...], w_ref[pl.ds(here, half), columns], preferred_element_type=F32
            ) + jnp.dot(
                far_ref[...], w_ref[pl.ds(there, half), columns], preferred_element_type=F32
            )
            for l in range(capacity):
                mine = slice(l * part, (l + 1) * part)
                other = slice(rows // 2 + l * part, rows // 2 + (l + 1) * part)
                keep_ref[mine, columns] = total[mine] * gate_ref[l]
                send_ref[mine, columns] = (total[other] * gate_ref[l]).astype(BF16)

    if streamed:
        resident = pl.BlockSpec((rows, half), lambda i: (0, 0))
        column = pl.BlockSpec((rows // 2, tile), lambda i: (0, i))
        specs = {
            "grid": (width // tile,),
            "in_specs": [SCALAR, SCALAR, resident, resident]
            + [pl.BlockSpec((2 * half, tile), lambda i: (0, i + first // tile))],
            "out_specs": [column, column],
            "compiler_params": params(44),
        }
    else:
        specs = {
            "in_specs": [SCALAR, SCALAR, INSIDE, INSIDE, INSIDE],
            "out_specs": [INSIDE, INSIDE],
            "compiler_params": params(),
        }
    return pl.pallas_call(
        kernel,
        out_shape=[
            jax.ShapeDtypeStruct((rows // 2, width), F32),
            jax.ShapeDtypeStruct((rows // 2, width), BF16),
        ],
        cost_estimate=pl.CostEstimate(
            flops=4 * rows * half * width,
            bytes_accessed=4 * rows * half + 3 * rows * width,
            transcendentals=0,
        ),
        **specs,
    )(places, gates, hidden, far, w_down)


def join(kept, arrived):
    def kernel(kept_ref, arrived_ref, out_ref):
        out_ref[...] = (kept_ref[...] + arrived_ref[...].astype(F32)).astype(BF16)

    size = kept.shape[0] * kept.shape[1]
    return pl.pallas_call(
        kernel,
        out_shape=jax.ShapeDtypeStruct(kept.shape, BF16),
        in_specs=[INSIDE, INSIDE],
        out_specs=INSIDE,
        cost_estimate=pl.CostEstimate(flops=size, bytes_accessed=8 * size, transcendentals=0),
        compiler_params=params(),
    )(kept, arrived)


def share_out(kept, arrived, near, places, lines, rows, capacity):
    width = kept.shape[1]

    def kernel(place_ref, kept_ref, arrived_ref, near_ref, *out_refs):
        for k in range(lines):
            mine = place_ref[2 * capacity + 2 * k]
            other = place_ref[2 * capacity + 2 * k + 1]
            start = pl.multiple_of(jnp.minimum(mine, capacity - 1) * rows, rows)
            value = kept_ref[pl.ds(start, rows), :] + arrived_ref[pl.ds(start, rows), :].astype(F32)
            value = jnp.where(mine < capacity, value, 0.0)
            start = pl.multiple_of(jnp.minimum(other, capacity - 1) * rows, rows)
            more = near_ref[pl.ds(start, rows), :].astype(F32)
            value = value + jnp.where(other < capacity, more, 0.0)
            out_refs[k][...] = value.astype(out_refs[k].dtype)

    size = rows * width
    kinds = [F32] + [BF16] * (lines - 1)
    return pl.pallas_call(
        kernel,
        out_shape=[jax.ShapeDtypeStruct((rows, width), kind) for kind in kinds],
        in_specs=[SCALAR, INSIDE, INSIDE, INSIDE],
        out_specs=[INSIDE] * lines,
        cost_estimate=pl.CostEstimate(
            flops=8 * size, bytes_accessed=(8 * capacity + 10) * size, transcendentals=0
        ),
        compiler_params=params(),
    )(places, kept, arrived, near)


def homed(tokens, w_gate, w_up, w_down, routes, gate_values):
    seq_count = lax.axis_size("seq")
    lines, pairs, halves = seq_count // 4, 2, 2
    capacity = 3 * routes.shape[0] // 8
    rows, width = tokens.shape

    flip_y = [(s, s ^ 2) for s in range(seq_count)]
    flip_x = [(s, s ^ 1) for s in range(seq_count)]
    swap = [(0, 1), (1, 0)]

    def along_z(k):
        return [(s, (s + 4 * k) % seq_count) for s in range(seq_count)]

    step = width // D_CHUNKS
    held = []
    for j in range(D_CHUNKS):
        chunk = tokens[:, j * step : (j + 1) * step]
        held.append([chunk] + [lax.ppermute(chunk, "seq", along_z(k)) for k in range(1, lines)])

    places, gates = tables(routes, gate_values, lines, pairs, halves, capacity)

    own = []
    for j in range(D_CHUNKS):
        leave = pick(held[j], places, capacity, capacity, rows)
        came = lax.ppermute(leave, "seq", flip_y)
        own.append(pick(held[j], places, 0, capacity, rows, came))
    mate = [lax.ppermute(a, "seq", flip_x) for a in own]
    far = [lax.ppermute(a, "tensor", swap) for a in own]
    mate_far = [lax.ppermute(a, "tensor", swap) for a in mate]

    state = ()
    for j in range(D_CHUNKS):
        pieces = (own[j], far[j], mate[j], mate_far[j])
        state = gate_up(pieces, w_gate[0], w_up[0], places, j, 256, state)
    hidden = state
    hidden_far = lax.ppermute(hidden, "tensor", swap)

    step = width // C_CHUNKS
    kept, arrived = [], []
    for j in range(C_CHUNKS):
        keep, leave = down(hidden, hidden_far, w_down[0], places, gates, 256, j * step, step)
        kept.append(keep)
        arrived.append(lax.ppermute(leave, "seq", flip_x))
    results = []
    for j in range(C_CHUNKS):
        leave = join(kept[j], arrived[j])
        near = lax.ppermute(leave, "seq", flip_y)
        outgoing = share_out(kept[j], arrived[j], near, places, lines, rows, capacity)
        result = outgoing[0]
        for k in range(1, lines):
            result = result + lax.ppermute(outgoing[k], "seq", along_z(k)).astype(F32)
        results.append(result.astype(BF16))
    return jnp.concatenate(results, axis=1)


def solution(mesh):
    placed = (
        P("seq", "tensor"),
        P("seq", None, "tensor"),
        P("seq", None, "tensor"),
        P("seq", None, "tensor"),
        P(),
        P(),
    )
    seq_count, tensor_count = mesh.shape["seq"], mesh.shape["tensor"]
    shared_home = seq_count == 2 * E and tensor_count == 2

    def per_device(*arrays):
        return homed(*arrays) if shared_home else gathered(*arrays)

    return jax.shard_map(
        per_device, mesh=mesh, in_specs=placed, out_specs=P("seq", "tensor"), check_vma=False
    )
```

time: 357 us -> 135 us (0.38)
  waiting for transfers between devices: 286 us -> 60.9 us
  Pallas kernels: 0 us -> 43.5 us
  matrix products: 42.6 us -> 0 us
  starting transfers between devices: 0.12 us -> 25.8 us
  between operations: 13.2 us -> 0.15 us
  local copies, waits for them, and re-layouts: 12.2 us -> 2.49 us
    reduce_scatter x1 -> x0, waiting for transfers between devices: 182 us -> none  [per_device(): summed = lax.psum_scatter(scattered, 'seq', scatter_dimension=0, tiled=True)]
    all_gather x3 -> x0, waiting for transfers between devices: 103 us -> none  [the longest x1 78.5 us: per_device(): columns = lax.all_gather(tokens, 'seq', axis=0, tiled=True)]
    ppermute x0 -> x25, waiting for transfers between devices: none -> 60.9 us  [the longest x6 13.5 us: homed(): lax.ppermute(chunk, 'seq', along_z(k))]
    pallas_call x0 -> x13, Pallas kernels: none -> 43.5 us  [the longest x2 24.9 us: gate_up(): pl.pallas_call(kernel, out_shape=jax.ShapeDtypeStruct((rows, width), BF16...]
    dot_general x4 -> x0, matrix products: 42.6 us -> none  [the longest x1 13.2 us: per_device(): gate_sum = jnp.dot(full_rows, gate_cols, preferred_element_type=jnp.float32)]
    ppermute x0 -> x25, starting transfers between devices: none -> 25.8 us  [the longest x6 9.89 us: homed(): lax.ppermute(chunk, 'seq', along_z(k))]
    dot_general x1 -> x0, local copies, waits for them, and re-layouts: 8.08 us -> none  [per_device(): jnp.einsum('lb,lrd->brd', picked.astype(jnp.float32), weighted, precision...]
    gather x1 -> x0, local copies, waits for them, and re-layouts: 4.06 us -> none  [per_device(): columns.reshape(block_count, block_rows, feature_width)[block_index]]
  transfers between devices with their start and end apart: 4 -> 25, of which waited for: 4 -> 14; matrix products, arithmetic and copies ran while one was open for 0% -> 1% of each run, Pallas kernels for 0% -> 18%
where the time goes in v1:
time: 135 us; the launch traced here: 134 us
  waiting for transfers between devices  60.9 us (45%)
  Pallas kernels  43.5 us (32%)
  starting transfers between devices  25.8 us (19%)
  local copies, waits for them, and re-layouts  2.49 us (2%)
    pallas_call x2, Pallas kernels, gate_up(): pl.pallas_call(kernel, out_shape=jax.ShapeDtypeStruct((rows, width), BF16...  24.9 us
    ppermute x6, waiting for transfers between devices, homed(): lax.ppermute(chunk, 'seq', along_z(k))  13.5 us
    pallas_call x2, Pallas kernels, down(): pl.pallas_call(kernel, out_shape=[jax.ShapeDtypeStruct((rows // 2, width)...  12.9 us
    ppermute x2, waiting for transfers between devices, homed(): arrived.append(lax.ppermute(leave, 'seq', flip_x))  10.6 us
    ppermute x6, waiting for transfers between devices, homed(): result = result + lax.ppermute(outgoing[k], 'seq', along_z(k)).astype(F32)  10.6 us
    ppermute x6, starting transfers between devices, homed(): lax.ppermute(chunk, 'seq', along_z(k))  9.89 us
    ppermute x2, waiting for transfers between devices, homed(): came = lax.ppermute(leave, 'seq', flip_y)  9.04 us
    ppermute x2, waiting for transfers between devices, homed(): mate = [lax.ppermute(a, 'seq', flip_x) for a in own]  8.92 us
  transfers between devices with their start and end apart: 25, of which 14 were waited for; matrix products, arithmetic and copies ran while one was open for 1% of the time, Pallas kernels for 18%

profile of v1, /device:TPU:10, one launch (start us, length us, event | category | flops | bytes accessed | tf_op | source)
XLA Modules:
  0.0 133.7 jit_solution(5404098380839373014)
XLA Ops:
  0.0 1.0 fusion
  1.0 0.5 collective-permute-start.9
  1.5 2.6 %collective-permute-start.8 = (bf16[64,1024]{1,0:T(8,128)(2,1)S(1)}, bf16[64,1024]{1,0:T(8,128)(2,1)S(1)}, u32[]{:S(2)}, u32[]{:S(2)}) collective-permute-start(bf16[64,1024]{1,0:T(8,128)(2,1)S(1)} %get-tuple-element.37.refs_0_), channel_id=1, source_target_pairs={{0,16},{2,18},{4,20},{6,22},{8,24},{10,26},{12,28},{14,30},{16,0},... | collective-permute-start | bytes 393224 | tf_op jit(solution)/shard_map/ppermute | solution.py:320
  4.1 2.5 %collective-permute-start.7 = (bf16[64,1024]{1,0:T(8,128)(2,1)S(1)}, bf16[64,1024]{1,0:T(8,128)(2,1)S(1)}, u32[]{:S(2)}, u32[]{:S(2)}) collective-permute-start(bf16[64,1024]{1,0:T(8,128)(2,1)S(1)} %get-tuple-element.37.refs_0_), channel_id=1, source_target_pairs={{0,8},{2,10},{4,12},{6,14},{8,16},{10,18},{12,20},{14,22},{16,24},... | collective-permute-start | bytes 393224 | tf_op jit(solution)/shard_map/ppermute | solution.py:320
  6.6 0.8 copy.7.routes_ref
  7.3 0.8 copy.8.values_ref
  8.1 1.4 %shard_map.64 = (s32[15]{0:T(128)S(1)}, f32[3]{0:T(128)S(1)}) custom-call(s32[8,2]{1,0:T(8,128)S(1)} %copy.7.routes_ref, f32[8,2]{1,0:T(8,128)S(1)} %copy.8.values_ref), custom_call_target="tpu_custom_call" | custom-call | tf_op jit(solution)/shard_map/pallas_call | solution.py:101
  9.5 3.5 %collective-permute-done.8.refs_2_ = bf16[64,1024]{1,0:T(8,128)(2,1)S(1)} collective-permute-done((bf16[64,1024]{1,0:T(8,128)(2,1)S(1)}, bf16[64,1024]{1,0:T(8,128)(2,1)S(1)}, u32[]{:S(2)}, u32[]{:S(2)}) %collective-permute-start.8) | collective-permute-done | bytes 131104 | tf_op jit(solution)/shard_map/ppermute | solution.py:320
  13.0 2.0 %collective-permute-done.7.refs_1_ = bf16[64,1024]{1,0:T(8,128)(2,1)S(1)} collective-permute-done((bf16[64,1024]{1,0:T(8,128)(2,1)S(1)}, bf16[64,1024]{1,0:T(8,128)(2,1)S(1)}, u32[]{:S(2)}, u32[]{:S(2)}) %collective-permute-start.7) | collective-permute-done | bytes 131104 | tf_op jit(solution)/shard_map/ppermute | solution.py:320
  15.0 0.6 shard_map.67
  15.6 1.6 %collective-permute-start.10 = (bf16[192,1024]{1,0:T(8,128)(2,1)S(1)}, bf16[192,1024]{1,0:T(8,128)(2,1)S(1)}, u32[]{:S(2)}, u32[]{:S(2)}) collective-permute-start(bf16[192,1024]{1,0:T(8,128)(2,1)S(1)} %shard_map.67), channel_id=1, source_target_pairs={{0,4},{2,6},{4,0},{6,2},{8,12},{10,14},{12,8},{14,10},{16,20},{18,... | collective-permute-start | bytes 1179656 | tf_op jit(solution)/shard_map/ppermute | solution.py:327
  17.2 1.3 collective-permute-start.2
  18.6 2.6 %collective-permute-start.1 = (bf16[64,1024]{1,0:T(8,128)(2,1)S(1)}, bf16[64,1024]{1,0:T(8,128)(2,1)S(1)}, u32[]{:S(2)}, u32[]{:S(2)}) collective-permute-start(bf16[64,1024]{1,0:T(8,128)(2,1)S(1)} %get-tuple-element.38.refs_0_), channel_id=1, source_target_pairs={{0,16},{2,18},{4,20},{6,22},{8,24},{10,26},{12,28},{14,30},{16,0},... | collective-permute-start | bytes 393224 | tf_op jit(solution)/shard_map/ppermute | solution.py:320
  21.2 0.4 collective-permute-start
  21.6 7.8 %collective-permute-done.2.refs_3_ = bf16[64,1024]{1,0:T(8,128)(2,1)S(1)} collective-permute-done((bf16[64,1024]{1,0:T(8,128)(2,1)S(1)}, bf16[64,1024]{1,0:T(8,128)(2,1)S(1)}, u32[]{:S(2)}, u32[]{:S(2)}) %collective-permute-start.2) | collective-permute-done | bytes 131104 | tf_op jit(solution)/shard_map/ppermute | solution.py:320
  29.6 0.6 shard_map.65
  30.2 0.6 collective-permute-start.3
  30.8 0.7 shard_map.68.own_ref
  31.5 0.6 collective-permute-start.12
  32.1 9.0 %collective-permute-done.3.refs_4_ = bf16[192,1024]{1,0:T(8,128)(2,1)S(1)} collective-permute-done((bf16[192,1024]{1,0:T(8,128)(2,1)S(1)}, bf16[192,1024]{1,0:T(8,128)(2,1)S(1)}, u32[]{:S(2)}, u32[]{:S(2)}) %collective-permute-start.3) | collective-permute-done | bytes 393248 | tf_op jit(solution)/shard_map/ppermute | solution.py:327
  41.1 0.7 shard_map.66.own_ref
  41.8 0.6 collective-permute-start.5
  42.4 0.5 collective-permute-start.13
  42.9 8.9 %collective-permute-done.5.mate_ref = bf16[192,1024]{1,0:T(8,128)(2,1)S(1)} collective-permute-done((bf16[192,1024]{1,0:T(8,128)(2,1)S(1)}, bf16[192,1024]{1,0:T(8,128)(2,1)S(1)}, u32[]{:S(2)}, u32[]{:S(2)}) %collective-permute-start.5) | collective-permute-done | bytes 393248 | tf_op jit(solution)/shard_map/ppermute | solution.py:329
  51.8 12.4 %shard_map.69 = (f32[384,2048]{1,0:T(8,128)S(1)}, f32[384,2048]{1,0:T(8,128)S(1)}) custom-call(s32[15]{0:T(128)S(1)} %get-tuple-element.21.place_ref, bf16[192,1024]{1,0:T(8,128)(2,1)S(1)} %shard_map.68.own_ref, bf16[192,1024]{1,0:T(8,128)(2,1)S(1)} %collective-permute-done.11.far_ref, bf16[192,1024]{1,0:T(8,128)(2,1)S(1)} %collective-permute-done.12.mate_ref, ...), custom_call_target="tpu_custom_call" | custom-call | flops 6442450944 | bytes 24641536 | tf_op jit(solution)/shard_map/pallas_call | solution.py:184
  64.3 12.5 %shard_map.70.own_ref = bf16[384,2048]{1,0:T(8,128)(2,1)S(1)} custom-call(s32[15]{0:T(128)S(1)} %get-tuple-element.21.place_ref, bf16[192,1024]{1,0:T(8,128)(2,1)S(1)} %shard_map.66.own_ref, bf16[192,1024]{1,0:T(8,128)(2,1)S(1)} %collective-permute-done.4.far_ref, bf16[192,1024]{1,0:T(8,128)(2,1)S(1)} %collective-permute-done.5.mate_ref, ...), custom_call_target="tpu_custom_call" | custom-call | flops 6442450944 | bytes 24641536 | tf_op jit(solution)/shard_map/pallas_call | solution.py:184
  76.7 0.6 collective-permute-start.14
  77.3 3.0 %collective-permute-done.14.far_ref = bf16[384,2048]{1,0:T(8,128)(2,1)S(1)} collective-permute-done((bf16[384,2048]{1,0:T(8,128)(2,1)S(1)}, bf16[384,2048]{1,0:T(8,128)(2,1)S(1)}, u32[]{:S(2)}, u32[]{:S(2)}) %collective-permute-start.14) | collective-permute-done | bytes 1572896 | tf_op jit(solution)/shard_map/ppermute | solution.py:338
  80.3 6.5 %shard_map.74 = (f32[192,1024]{1,0:T(8,128)S(1)}, bf16[192,1024]{1,0:T(8,128)(2,1)S(1)}) custom-call(s32[15]{0:T(128)S(1)} %get-tuple-element.21.place_ref, f32[3]{0:T(128)S(1)} %get-tuple-element.22.gate_ref, bf16[384,2048]{1,0:T(8,128)(2,1)S(1)} %shard_map.70.own_ref, bf16[384,2048]{1,0:T(8,128)(2,1)S(1)} %collective-permute-done.14.far_ref, ...), custom_call_target="tpu_custom_call" | custom-call | flops 3221225472 | bytes 4325376 | tf_op jit(solution)/shard_map/pallas_call | solution.py:244
  86.8 0.6 collective-permute-start.20
  87.4 6.4 %shard_map.71 = (f32[192,1024]{1,0:T(8,128)S(1)}, bf16[192,1024]{1,0:T(8,128)(2,1)S(1)}) custom-call(s32[15]{0:T(128)S(1)} %get-tuple-element.21.place_ref, f32[3]{0:T(128)S(1)} %get-tuple-element.22.gate_ref, bf16[384,2048]{1,0:T(8,128)(2,1)S(1)} %shard_map.70.own_ref, bf16[384,2048]{1,0:T(8,128)(2,1)S(1)} %collective-permute-done.14.far_ref, ...), custom_call_target="tpu_custom_call" | custom-call | flops 3221225472 | bytes 4325376 | tf_op jit(solution)/shard_map/pallas_call | solution.py:244
  93.9 1.6 %collective-permute-start.15 = (bf16[192,1024]{1,0:T(8,128)(2,1)S(1)}, bf16[192,1024]{1,0:T(8,128)(2,1)S(1)}, u32[]{:S(2)}, u32[]{:S(2)}) collective-permute-start(bf16[192,1024]{1,0:T(8,128)(2,1)S(1)} %get-tuple-element.26), channel_id=1, source_target_pairs={{0,2},{2,0},{4,6},{6,4},{8,10},{10,8},{12,14},{14,12},{16,18},{18,... | collective-permute-start | bytes 1179656 | tf_op jit(solution)/shard_map/ppermute | solution.py:345
  95.4 3.4 %collective-permute-done.20.arrived_ref = bf16[192,1024]{1,0:T(8,128)(2,1)S(1)} collective-permute-done((bf16[192,1024]{1,0:T(8,128)(2,1)S(1)}, bf16[192,1024]{1,0:T(8,128)(2,1)S(1)}, u32[]{:S(2)}, u32[]{:S(2)}) %collective-permute-start.20) | collective-permute-done | bytes 393248 | tf_op jit(solution)/shard_map/ppermute | solution.py:345
  98.9 0.6 collective-permute-start.21
  99.5 7.2 %collective-permute-done.15.arrived_ref = bf16[192,1024]{1,0:T(8,128)(2,1)S(1)} collective-permute-done((bf16[192,1024]{1,0:T(8,128)(2,1)S(1)}, bf16[192,1024]{1,0:T(8,128)(2,1)S(1)}, u32[]{:S(2)}, u32[]{:S(2)}) %collective-permute-start.15) | collective-permute-done | bytes 393248 | tf_op jit(solution)/shard_map/ppermute | solution.py:345
  106.8 0.6 collective-permute-start.16
  107.4 1.6 %collective-permute-done.21.near_ref = bf16[192,1024]{1,0:T(8,128)(2,1)S(1)} collective-permute-done((bf16[192,1024]{1,0:T(8,128)(2,1)S(1)}, bf16[192,1024]{1,0:T(8,128)(2,1)S(1)}, u32[]{:S(2)}, u32[]{:S(2)}) %collective-permute-start.21) | collective-permute-done | bytes 393248 | tf_op jit(solution)/shard_map/ppermute | solution.py:349
  108.9 0.8 shard_map.76
  109.7 2.5 %collective-permute-start.22 = (bf16[64,1024]{1,0:T(8,128)(2,1)S(1)}, bf16[64,1024]{1,0:T(8,128)(2,1)S(1)}, u32[]{:S(2)}, u32[]{:S(2)}) collective-permute-start(bf16[64,1024]{1,0:T(8,128)(2,1)S(1)} %get-tuple-element.34), channel_id=1, source_target_pairs={{0,8},{2,10},{4,12},{6,14},{8,16},{10,18},{12,20},{14,22},{16,24},... | collective-permute-start | bytes 393224 | tf_op jit(solution)/shard_map/ppermute | solution.py:353
  112.3 1.5 %collective-permute-start.24 = (bf16[64,1024]{1,0:T(8,128)(2,1)S(1)}, bf16[64,1024]{1,0:T(8,128)(2,1)S(1)}, u32[]{:S(2)}, u32[]{:S(2)}) collective-permute-start(bf16[64,1024]{1,0:T(8,128)(2,1)S(1)} %get-tuple-element.36), channel_id=1, source_target_pairs={{0,24},{2,26},{4,28},{6,30},{8,0},{10,2},{12,4},{14,6},{16,8},{18,... | collective-permute-start | bytes 393224 | tf_op jit(solution)/shard_map/ppermute | solution.py:353
  113.8 3.6 %collective-permute-done.16.near_ref = bf16[192,1024]{1,0:T(8,128)(2,1)S(1)} collective-permute-done((bf16[192,1024]{1,0:T(8,128)(2,1)S(1)}, bf16[192,1024]{1,0:T(8,128)(2,1)S(1)}, u32[]{:S(2)}, u32[]{:S(2)}) %collective-permute-start.16) | collective-permute-done | bytes 393248 | tf_op jit(solution)/shard_map/ppermute | solution.py:349
  117.4 0.8 shard_map.73
  118.2 2.5 %collective-permute-start.17 = (bf16[64,1024]{1,0:T(8,128)(2,1)S(1)}, bf16[64,1024]{1,0:T(8,128)(2,1)S(1)}, u32[]{:S(2)}, u32[]{:S(2)}) collective-permute-start(bf16[64,1024]{1,0:T(8,128)(2,1)S(1)} %get-tuple-element.28), channel_id=1, source_target_pairs={{0,8},{2,10},{4,12},{6,14},{8,16},{10,18},{12,20},{14,22},{16,24},... | collective-permute-start | bytes 393224 | tf_op jit(solution)/shard_map/ppermute | solution.py:353
  120.7 1.5 %collective-permute-start.19 = (bf16[64,1024]{1,0:T(8,128)(2,1)S(1)}, bf16[64,1024]{1,0:T(8,128)(2,1)S(1)}, u32[]{:S(2)}, u32[]{:S(2)}) collective-permute-start(bf16[64,1024]{1,0:T(8,128)(2,1)S(1)} %get-tuple-element.30), channel_id=1, source_target_pairs={{0,24},{2,26},{4,28},{6,30},{8,0},{10,2},{12,4},{14,6},{16,8},{18,... | collective-permute-start | bytes 393224 | tf_op jit(solution)/shard_map/ppermute | solution.py:353
  122.2 6.5 %collective-permute-done.23 = bf16[64,1024]{1,0:T(8,128)(2,1)S(1)} collective-permute-done((bf16[64,1024]{1,0:T(8,128)(2,1)S(1)}, bf16[64,1024]{1,0:T(8,128)(2,1)S(1)}, u32[]{:S(2)}, u32[]{:S(2)}) %collective-permute-start.23) | collective-permute-done | bytes 131104 | tf_op jit(solution)/shard_map/ppermute | solution.py:353
  128.9 2.6 %collective-permute-done.17 = bf16[64,1024]{1,0:T(8,128)(2,1)S(1)} collective-permute-done((bf16[64,1024]{1,0:T(8,128)(2,1)S(1)}, bf16[64,1024]{1,0:T(8,128)(2,1)S(1)}, u32[]{:S(2)}, u32[]{:S(2)}) %collective-permute-start.17) | collective-permute-done | bytes 131104 | tf_op jit(solution)/shard_map/ppermute | solution.py:353
  131.5 1.4 %collective-permute-done.18 = bf16[64,1024]{1,0:T(8,128)(2,1)S(1)} collective-permute-done((bf16[64,1024]{1,0:T(8,128)(2,1)S(1)}, bf16[64,1024]{1,0:T(8,128)(2,1)S(1)}, u32[]{:S(2)}, u32[]{:S(2)}) %collective-permute-start.18) | collective-permute-done | bytes 131104 | tf_op jit(solution)/shard_map/ppermute | solution.py:353
  133.0 0.7 pad_maximum_fusion
  (21 shorter events, 0.5 us)
Async XLA Ops:
  1.0 8.5 %collective-permute-start.9 = (bf16[64,1024]{1,0:T(8,128)(2,1)S(1)}, bf16[64,1024]{1,0:T(8,128)(2,1)S(1)}, u32[]{:S(2)}, u32[]{:S(2)}) collective-permute-start(bf16[64,1024]{1,0:T(8,128)(2,1)S(1)} %get-tuple-element.37.refs_0_), channel_id=1, source_target_pairs={{0,24},{2,26},{4,28},{6,30},{8,0},{10,2},{12,4},{14,6},{16,8},{18,... | collective-permute-start | bytes 393224 | tf_op jit(solution)/shard_map/ppermute | solution.py:320
  1.5 11.5 %collective-permute-start.8 = (bf16[64,1024]{1,0:T(8,128)(2,1)S(1)}, bf16[64,1024]{1,0:T(8,128)(2,1)S(1)}, u32[]{:S(2)}, u32[]{:S(2)}) collective-permute-start(bf16[64,1024]{1,0:T(8,128)(2,1)S(1)} %get-tuple-element.37.refs_0_), channel_id=1, source_target_pairs={{0,16},{2,18},{4,20},{6,22},{8,24},{10,26},{12,28},{14,30},{16,0},... | collective-permute-start | bytes 393224 | tf_op jit(solution)/shard_map/ppermute | solution.py:320
  4.1 10.9 %collective-permute-start.7 = (bf16[64,1024]{1,0:T(8,128)(2,1)S(1)}, bf16[64,1024]{1,0:T(8,128)(2,1)S(1)}, u32[]{:S(2)}, u32[]{:S(2)}) collective-permute-start(bf16[64,1024]{1,0:T(8,128)(2,1)S(1)} %get-tuple-element.37.refs_0_), channel_id=1, source_target_pairs={{0,8},{2,10},{4,12},{6,14},{8,16},{10,18},{12,20},{14,22},{16,24},... | collective-permute-start | bytes 393224 | tf_op jit(solution)/shard_map/ppermute | solution.py:320
  15.6 15.2 %collective-permute-start.10 = (bf16[192,1024]{1,0:T(8,128)(2,1)S(1)}, bf16[192,1024]{1,0:T(8,128)(2,1)S(1)}, u32[]{:S(2)}, u32[]{:S(2)}) collective-permute-start(bf16[192,1024]{1,0:T(8,128)(2,1)S(1)} %shard_map.67), channel_id=1, source_target_pairs={{0,4},{2,6},{4,0},{6,2},{8,12},{10,14},{12,8},{14,10},{16,20},{18,... | collective-permute-start | bytes 1179656 | tf_op jit(solution)/shard_map/ppermute | solution.py:327
  17.2 12.2 %collective-permute-start.2 = (bf16[64,1024]{1,0:T(8,128)(2,1)S(1)}, bf16[64,1024]{1,0:T(8,128)(2,1)S(1)}, u32[]{:S(2)}, u32[]{:S(2)}) collective-permute-start(bf16[64,1024]{1,0:T(8,128)(2,1)S(1)} %get-tuple-element.38.refs_0_), channel_id=1, source_target_pairs={{0,24},{2,26},{4,28},{6,30},{8,0},{10,2},{12,4},{14,6},{16,8},{18,... | collective-permute-start | bytes 393224 | tf_op jit(solution)/shard_map/ppermute | solution.py:320
  18.6 10.8 %collective-permute-start.1 = (bf16[64,1024]{1,0:T(8,128)(2,1)S(1)}, bf16[64,1024]{1,0:T(8,128)(2,1)S(1)}, u32[]{:S(2)}, u32[]{:S(2)}) collective-permute-start(bf16[64,1024]{1,0:T(8,128)(2,1)S(1)} %get-tuple-element.38.refs_0_), channel_id=1, source_target_pairs={{0,16},{2,18},{4,20},{6,22},{8,24},{10,26},{12,28},{14,30},{16,0},... | collective-permute-start | bytes 393224 | tf_op jit(solution)/shard_map/ppermute | solution.py:320
  21.2 8.4 %collective-permute-start = (bf16[64,1024]{1,0:T(8,128)(2,1)S(1)}, bf16[64,1024]{1,0:T(8,128)(2,1)S(1)}, u32[]{:S(2)}, u32[]{:S(2)}) collective-permute-start(bf16[64,1024]{1,0:T(8,128)(2,1)S(1)} %get-tuple-element.38.refs_0_), channel_id=1, source_target_pairs={{0,8},{2,10},{4,12},{6,14},{8,16},{10,18},{12,20},{14,22},{16,24},... | collective-permute-start | bytes 393224 | tf_op jit(solution)/shard_map/ppermute | solution.py:320
  30.2 10.9 %collective-permute-start.3 = (bf16[192,1024]{1,0:T(8,128)(2,1)S(1)}, bf16[192,1024]{1,0:T(8,128)(2,1)S(1)}, u32[]{:S(2)}, u32[]{:S(2)}) collective-permute-start(bf16[192,1024]{1,0:T(8,128)(2,1)S(1)} %shard_map.65), channel_id=1, source_target_pairs={{0,4},{2,6},{4,0},{6,2},{8,12},{10,14},{12,8},{14,10},{16,20},{18,... | collective-permute-start | bytes 1179656 | tf_op jit(solution)/shard_map/ppermute | solution.py:327
  31.5 10.9 %collective-permute-start.12 = (bf16[192,1024]{1,0:T(8,128)(2,1)S(1)}, bf16[192,1024]{1,0:T(8,128)(2,1)S(1)}, u32[]{:S(2)}, u32[]{:S(2)}) collective-permute-start(bf16[192,1024]{1,0:T(8,128)(2,1)S(1)} %shard_map.68.own_ref), channel_id=1, source_target_pairs={{0,2},{2,0},{4,6},{6,4},{8,10},{10,8},{12,14},{14,12},{16,18},{18,... | collective-permute-start | bytes 1179656 | tf_op jit(solution)/shard_map/ppermute | solution.py:329
  41.8 10.0 %collective-permute-start.5 = (bf16[192,1024]{1,0:T(8,128)(2,1)S(1)}, bf16[192,1024]{1,0:T(8,128)(2,1)S(1)}, u32[]{:S(2)}, u32[]{:S(2)}) collective-permute-start(bf16[192,1024]{1,0:T(8,128)(2,1)S(1)} %shard_map.66.own_ref), channel_id=1, source_target_pairs={{0,2},{2,0},{4,6},{6,4},{8,10},{10,8},{12,14},{14,12},{16,18},{18,... | collective-permute-start | bytes 1179656 | tf_op jit(solution)/shard_map/ppermute | solution.py:329
  42.4 9.4 %collective-permute-start.11 = (bf16[192,1024]{1,0:T(8,128)(2,1)S(1)}, bf16[192,1024]{1,0:T(8,128)(2,1)S(1)}, u32[]{:S(2)}, u32[]{:S(2)}) collective-permute-start(bf16[192,1024]{1,0:T(8,128)(2,1)S(1)} %shard_map.68.own_ref), channel_id=1, source_target_pairs={{0,1},{1,0},{2,3},{3,2},{4,5},{5,4},{6,7},{7,6},{8,9},{9,8},{10,11... | collective-permute-start | bytes 1179656 | tf_op jit(solution)/shard_map/ppermute | solution.py:330
  42.4 9.4 %collective-permute-start.13 = (bf16[192,1024]{1,0:T(8,128)(2,1)S(1)}, bf16[192,1024]{1,0:T(8,128)(2,1)S(1)}, u32[]{:S(2)}, u32[]{:S(2)}) collective-permute-start(bf16[192,1024]{1,0:T(8,128)(2,1)S(1)} %collective-permute-done.12.mate_ref), channel_id=1, source_target_pairs={{0,1},{1,0},{2,3},{3,2},{4,5},{5,4},{6,7},{7,6},{8,9},{9,8},{10,11... | collective-permute-start | bytes 1179656 | tf_op jit(solution)/shard_map/ppermute | solution.py:331
  42.9 21.3 %collective-permute-start.4 = (bf16[192,1024]{1,0:T(8,128)(2,1)S(1)}, bf16[192,1024]{1,0:T(8,128)(2,1)S(1)}, u32[]{:S(2)}, u32[]{:S(2)}) collective-permute-start(bf16[192,1024]{1,0:T(8,128)(2,1)S(1)} %shard_map.66.own_ref), channel_id=1, source_target_pairs={{0,1},{1,0},{2,3},{3,2},{4,5},{5,4},{6,7},{7,6},{8,9},{9,8},{10,11... | collective-permute-start | bytes 1179656 | tf_op jit(solution)/shard_map/ppermute | solution.py:330
  51.8 12.4 %collective-permute-start.6 = (bf16[192,1024]{1,0:T(8,128)(2,1)S(1)}, bf16[192,1024]{1,0:T(8,128)(2,1)S(1)}, u32[]{:S(2)}, u32[]{:S(2)}) collective-permute-start(bf16[192,1024]{1,0:T(8,128)(2,1)S(1)} %collective-permute-done.5.mate_ref), channel_id=1, source_target_pairs={{0,1},{1,0},{2,3},{3,2},{4,5},{5,4},{6,7},{7,6},{8,9},{9,8},{10,11... | collective-permute-start | bytes 1179656 | tf_op jit(solution)/shard_map/ppermute | solution.py:331
  76.7 3.6 %collective-permute-start.14 = (bf16[384,2048]{1,0:T(8,128)(2,1)S(1)}, bf16[384,2048]{1,0:T(8,128)(2,1)S(1)}, u32[]{:S(2)}, u32[]{:S(2)}) collective-permute-start(bf16[384,2048]{1,0:T(8,128)(2,1)S(1)} %shard_map.70.own_ref), channel_id=1, source_target_pairs={{0,1},{1,0},{2,3},{3,2},{4,5},{5,4},{6,7},{7,6},{8,9},{9,8},{10,11... | collective-permute-start | bytes 4718600 | tf_op jit(solution)/shard_map/ppermute | solution.py:338
  86.8 12.1 %collective-permute-start.20 = (bf16[192,1024]{1,0:T(8,128)(2,1)S(1)}, bf16[192,1024]{1,0:T(8,128)(2,1)S(1)}, u32[]{:S(2)}, u32[]{:S(2)}) collective-permute-start(bf16[192,1024]{1,0:T(8,128)(2,1)S(1)} %get-tuple-element.32), channel_id=1, source_target_pairs={{0,2},{2,0},{4,6},{6,4},{8,10},{10,8},{12,14},{14,12},{16,18},{18,... | collective-permute-start | bytes 1179656 | tf_op jit(solution)/shard_map/ppermute | solution.py:345
  93.9 12.8 %collective-permute-start.15 = (bf16[192,1024]{1,0:T(8,128)(2,1)S(1)}, bf16[192,1024]{1,0:T(8,128)(2,1)S(1)}, u32[]{:S(2)}, u32[]{:S(2)}) collective-permute-start(bf16[192,1024]{1,0:T(8,128)(2,1)S(1)} %get-tuple-element.26), channel_id=1, source_target_pairs={{0,2},{2,0},{4,6},{6,4},{8,10},{10,8},{12,14},{14,12},{16,18},{18,... | collective-permute-start | bytes 1179656 | tf_op jit(solution)/shard_map/ppermute | solution.py:345
  98.9 10.0 %collective-permute-start.21 = (bf16[192,1024]{1,0:T(8,128)(2,1)S(1)}, bf16[192,1024]{1,0:T(8,128)(2,1)S(1)}, u32[]{:S(2)}, u32[]{:S(2)}) collective-permute-start(bf16[192,1024]{1,0:T(8,128)(2,1)S(1)} %shard_map.75), channel_id=1, source_target_pairs={{0,4},{2,6},{4,0},{6,2},{8,12},{10,14},{12,8},{14,10},{16,20},{18,... | collective-permute-start | bytes 1179656 | tf_op jit(solution)/shard_map/ppermute | solution.py:349
  106.8 10.6 %collective-permute-start.16 = (bf16[192,1024]{1,0:T(8,128)(2,1)S(1)}, bf16[192,1024]{1,0:T(8,128)(2,1)S(1)}, u32[]{:S(2)}, u32[]{:S(2)}) collective-permute-start(bf16[192,1024]{1,0:T(8,128)(2,1)S(1)} %shard_map.72), channel_id=1, source_target_pairs={{0,4},{2,6},{4,0},{6,2},{8,12},{10,14},{12,8},{14,10},{16,20},{18,... | collective-permute-start | bytes 1179656 | tf_op jit(solution)/shard_map/ppermute | solution.py:349
  109.7 11.0 %collective-permute-start.22 = (bf16[64,1024]{1,0:T(8,128)(2,1)S(1)}, bf16[64,1024]{1,0:T(8,128)(2,1)S(1)}, u32[]{:S(2)}, u32[]{:S(2)}) collective-permute-start(bf16[64,1024]{1,0:T(8,128)(2,1)S(1)} %get-tuple-element.34), channel_id=1, source_target_pairs={{0,8},{2,10},{4,12},{6,14},{8,16},{10,18},{12,20},{14,22},{16,24},... | collective-permute-start | bytes 393224 | tf_op jit(solution)/shard_map/ppermute | solution.py:353
  112.3 16.5 %collective-permute-start.23 = (bf16[64,1024]{1,0:T(8,128)(2,1)S(1)}, bf16[64,1024]{1,0:T(8,128)(2,1)S(1)}, u32[]{:S(2)}, u32[]{:S(2)}) collective-permute-start(bf16[64,1024]{1,0:T(8,128)(2,1)S(1)} %get-tuple-element.35), channel_id=1, source_target_pairs={{0,16},{2,18},{4,20},{6,22},{8,24},{10,26},{12,28},{14,30},{16,0},... | collective-permute-start | bytes 393224 | tf_op jit(solution)/shard_map/ppermute | solution.py:353
  112.3 16.5 %collective-permute-start.24 = (bf16[64,1024]{1,0:T(8,128)(2,1)S(1)}, bf16[64,1024]{1,0:T(8,128)(2,1)S(1)}, u32[]{:S(2)}, u32[]{:S(2)}) collective-permute-start(bf16[64,1024]{1,0:T(8,128)(2,1)S(1)} %get-tuple-element.36), channel_id=1, source_target_pairs={{0,24},{2,26},{4,28},{6,30},{8,0},{10,2},{12,4},{14,6},{16,8},{18,... | collective-permute-start | bytes 393224 | tf_op jit(solution)/shard_map/ppermute | solution.py:353
  118.2 13.3 %collective-permute-start.17 = (bf16[64,1024]{1,0:T(8,128)(2,1)S(1)}, bf16[64,1024]{1,0:T(8,128)(2,1)S(1)}, u32[]{:S(2)}, u32[]{:S(2)}) collective-permute-start(bf16[64,1024]{1,0:T(8,128)(2,1)S(1)} %get-tuple-element.28), channel_id=1, source_target_pairs={{0,8},{2,10},{4,12},{6,14},{8,16},{10,18},{12,20},{14,22},{16,24},... | collective-permute-start | bytes 393224 | tf_op jit(solution)/shard_map/ppermute | solution.py:353
  120.7 12.2 %collective-permute-start.18 = (bf16[64,1024]{1,0:T(8,128)(2,1)S(1)}, bf16[64,1024]{1,0:T(8,128)(2,1)S(1)}, u32[]{:S(2)}, u32[]{:S(2)}) collective-permute-start(bf16[64,1024]{1,0:T(8,128)(2,1)S(1)} %get-tuple-element.29), channel_id=1, source_target_pairs={{0,16},{2,18},{4,20},{6,22},{8,24},{10,26},{12,28},{14,30},{16,0},... | collective-permute-start | bytes 393224 | tf_op jit(solution)/shard_map/ppermute | solution.py:353
  120.7 12.2 %collective-permute-start.19 = (bf16[64,1024]{1,0:T(8,128)(2,1)S(1)}, bf16[64,1024]{1,0:T(8,128)(2,1)S(1)}, u32[]{:S(2)}, u32[]{:S(2)}) collective-permute-start(bf16[64,1024]{1,0:T(8,128)(2,1)S(1)} %get-tuple-element.30), channel_id=1, source_target_pairs={{0,24},{2,26},{4,28},{6,30},{8,0},{10,2},{12,4},{14,6},{16,8},{18,... | collective-permute-start | bytes 393224 | tf_op jit(solution)/shard_map/ppermute | solution.py:353
